TPU v7x, 32 devices: a whole 2x2x4 slice. The times are simulated.
32 devices in a mesh: groups: 2 (over x), dp: 16 (over z, y, core).
Axes of the slice: x: 2, y: 2, z: 4, core: 2. Of those that a mesh axis runs over, the one named last changes fastest.
Arguments:
- tokens: bfloat16 [12288, 8192], P(('groups', 'dp')), parts along dimension 0, may hold values from -6 to 6
- base_weight: bfloat16 [8192, 768], P('dp'), may hold values from -0.0625 to 0.0625
- down_stack: bfloat16 [8192, 512], P('dp'), may hold values from -0.0625 to 0.0625
- up_stack: bfloat16 [512, 768], replicated, may hold values from -0.75 to 0.75
- adapter_scale: float32 [8], replicated, may hold values from 0.5 to 2
- lengths: int32 [64], P(('groups', 'dp')), parts along dimension 0, may hold values from 1 to 256, as said below
- adapter_ids: int32 [64], P(('groups', 'dp')), parts along dimension 0, may hold values from 0 to 7
Outputs:
- projected: bfloat16 [12288, 768], P(('groups', 'dp')), parts along dimension 0
There are 2 independent parts, one for each index of `groups`. A program takes and returns all parts, laid end to end along the dimension named above; an argument that names none is the same for every part. Nothing has to cross between parts.
Inputs may be any that keep to these rules, and one draw needn't show every extreme that they name: `lengths`: each index of dp holds two requests whose block counts ceil(length / 128) add up to exactly 3.
All inputs are finite; a program needn't handle non-finite values.
Results may differ from a plain program's by a relative error of at most 0.0042.
Values may be sent and summed in bfloat16 or wider, within the bound.
A program may use at most 128 MiB of HBM per device.

v0:
```python
import jax
import jax.numpy as jnp
from jax import lax
from jax.sharding import PartitionSpec as P

RANK = 64
BLOCK = 128


def layout(lengths, adapter_ids, row_count):
    counts = (lengths + BLOCK - 1) // BLOCK
    position = jnp.arange(row_count, dtype=jnp.int32)
    boundary = counts[0] * BLOCK
    second = position >= boundary
    offset = jnp.where(second, position - boundary, position)
    is_live = offset < jnp.where(second, lengths[1], lengths[0])
    token_adapter = jnp.where(second, adapter_ids[1], adapter_ids[0])
    return (is_live, token_adapter)


def local(tokens, base_weight, down_stack, up_stack, adapter_scale, lengths, adapter_ids):
    row_count = tokens.shape[0]
    num_blocks = row_count // BLOCK
    adapters = down_stack.shape[1] // RANK
    is_live, token_adapter = layout(lengths, adapter_ids, row_count)
    adapter_per_block = token_adapter.reshape(num_blocks, BLOCK)[:, 0]
    w_piece = lax.all_gather(base_weight, "dp", axis=0, tiled=True)
    a_piece = lax.all_gather(down_stack, "dp", axis=0, tiled=True)
    width_dev = w_piece.shape[0]
    base_projection_share = jnp.dot(tokens, w_piece, preferred_element_type=jnp.float32)
    down_split = a_piece.reshape(width_dev, adapters, RANK)
    selected_adapter = jnp.take(down_split, adapter_per_block, axis=1)
    token_block_groups = tokens.reshape(num_blocks, BLOCK, width_dev)
    low_part = jnp.einsum(
        "wmu,uwi->wmi", token_block_groups, selected_adapter, preferred_element_type=jnp.float32
    )
    low_rank = low_part.reshape(row_count, RANK)
    low_rank = low_rank.astype(jnp.bfloat16)
    onehot = token_adapter[:, None] == jnp.arange(adapters, dtype=jnp.int32)[None, :]
    widened = jnp.where(
        onehot[:, :, None], low_rank[:, None, :], jnp.zeros((), jnp.bfloat16)
    ).reshape(row_count, adapters * RANK)
    adapter_out = jnp.dot(widened, up_stack, preferred_element_type=jnp.float32)
    token_scale = jnp.sum(jnp.where(onehot, adapter_scale[None, :], 0.0), axis=1)
    result = jnp.where(
        is_live[:, None], base_projection_share + token_scale[:, None] * adapter_out, 0.0
    )
    return result.astype(jnp.bfloat16)


def solution(mesh):
    in_specs = (
        P(("groups", "dp"), None),
        P("dp", None),
        P("dp", None),
        P(),
        P(),
        P(("groups", "dp")),
        P(("groups", "dp")),
    )
    out_specs = P(("groups", "dp"), None)
    return jax.shard_map(local, mesh=mesh, in_specs=in_specs, out_specs=out_specs, check_vma=False)
```

profile of v0, /device:TPU:0, one launch (start us, length us, event | category | flops | bytes accessed | tf_op | source)
XLA Modules:
  0.0 209.0 jit_solution(384807473434805781)
XLA Ops:
  6.5 0.0 copy-start
  6.5 0.0 all-gather.5.cloned.1.call-start
  6.5 2.1 %copy.8 = bf16[512,512]{0,1:T(8,128)(2,1)} copy(bf16[512,512]{1,0:T(8,128)(2,1)} %param.9) | data formatting | bytes 1048576 | tf_op args[2]
  8.7 0.0 all-gather.5.cloned.1.call-update
  8.7 0.0 all-gather.3.cloned.1.call-start
  8.7 0.7 all-gather.3.cloned.1.call-update
  9.4 0.7 and_select_fusion
  10.1 1.3 fusion.18
  11.5 1.2 and_bitcast_fusion
  12.7 1.2 fusion.16
  14.0 1.4 fusion.17
  15.3 1.2 select_compare_fusion
  16.6 1.2 fusion.14
  17.8 0.7 select_reduce_fusion
  18.6 71.4 %all-gather.5.cloned.1.call-done = bf16[8192,512]{0,1:T(8,128)(2,1)} async-done(((bf16[512,512]{0,1:T(8,128)(2,1)}), bf16[8192,512]{0,1:T(8,128)(2,1)}) %all-gather.5.cloned.1.call-update) | async-done | bytes 8388624 | tf_op jit(solution)/shard_map/all_gather | solution.py:28
  90.0 5.9 %gather_fusion = bf16[3,8192,64]{1,2,0:T(8,128)(2,1)} fusion(bf16[8192,8,64]{0,2,1:T(8,128)(2,1)} %bitcast.31, s32[1024]{0:T(1024)S(1)} %pad_clamp_fusion), kind=kCustom, calls=%fused_computation | custom fusion | bytes 6291468 | tf_op jit(solution)/shard_map/jit(_take)/gather | solution.py:32
  95.9 6.7 %fusion.11 = bf16[3,8,8,128]{3,2,1,0:T(8,128)(2,1)S(1)} fusion(bf16[3,128,8192]{2,1,0:T(8,128)(2,1)} %bitcast.34, bf16[3,8192,64]{1,2,0:T(8,128)(2,1)} %gather_fusion, pred[3]{0:T(512)(128)(4,1)S(1)} %and_bitcast_fusion), kind=kOutput, calls=%fused_computation.11 | convolution fusion | flops 404250624 | bytes 9486339 | tf_op jit(solution)/shard_map/wmu,uwi->wmi/dot_general | solution.py:34
  102.5 0.1 broadcast_select_fusion
  102.6 88.3 %all-gather.3.cloned.1.call-done = bf16[8192,768]{1,0:T(8,128)(2,1)} async-done(((bf16[512,768]{1,0:T(8,128)(2,1)}), bf16[8192,768]{1,0:T(8,128)(2,1)}) %all-gather.3.cloned.1.call-update) | async-done | bytes 12582928 | tf_op jit(solution)/shard_map/all_gather | solution.py:27
  190.9 9.9 %fusion.19 = f32[384,768]{1,0:T(8,128)S(1)} fusion(bf16[384,8192]{1,0:T(8,128)(2,1)} %param.7, bf16[8192,768]{1,0:T(8,128)(2,1)} %all-gather.3.cloned.1.call-done), kind=kOutput, calls=%fused_computation.33 | convolution fusion | flops 4831838208 | bytes 20054016 | tf_op jit(solution)/shard_map/dot_general | solution.py:30
  200.8 0.0 copy-done
  200.8 1.3 fusion.7
  (3 shorter events, 0.0 us)
Async XLA Ops:
  6.5 194.3 %copy-start = (bf16[512,768]{1,0:T(8,128)(2,1)S(1)}, bf16[512,768]{1,0:T(8,128)(2,1)}, u32[]{:S(2)}) copy-start(bf16[512,768]{1,0:T(8,128)(2,1)} %param.10) | copy-start | bytes 2359300
  6.5 83.4 %all-gather.5.cloned.1.call-start = ((), (), s32[]{:S(2)}) async-start(), calls=%async_computation.1 | async-start | bytes 8912896 | tf_op jit(solution)/shard_map/all_gather | solution.py:28
  8.7 182.2 %all-gather.3.cloned.1.call-start = ((), (), s32[]{:S(2)}) async-start(), calls=%async_computation | async-start | bytes 13369344 | tf_op jit(solution)/shard_map/all_gather | solution.py:27
Sparse Core Ops, SparseCore 0:
  9.5 80.4 all-gather.4
  92.2 98.5 all-gather.2
where the time goes:
time: 209 us
  waiting for transfers between devices  160 us (77%)
  matrix products  17.9 us (9%)
  between operations  13.5 us (6%)
  local copies, waits for them, and re-layouts  10.8 us (5%)
  other arithmetic  6.4 us (3%)
    all_gather x1, waiting for transfers between devices, local(): w_piece = lax.all_gather(base_weight, 'dp', axis=0, tiled=True)  88.3 us
    all_gather x1, waiting for transfers between devices, local(): a_piece = lax.all_gather(down_stack, 'dp', axis=0, tiled=True)  71.4 us
    dot_general x1, matrix products, local(): jnp.dot(tokens, w_piece, preferred_element_type=jnp.float32)  9.92 us
    dot_general x1, matrix products, local(): jnp.einsum('wmu,uwi->wmi', token_block_groups, selected_adapter, preferre...  6.65 us
    gather x1, local copies, waits for them, and re-layouts, local(): selected_adapter = jnp.take(down_split, adapter_per_block, axis=1)  5.9 us
  transfers between devices with their start and end apart: 2, of which 2 were waited for; matrix products, arithmetic and copies ran while one was open for 10% of the time, Pallas kernels for 0%

commit v1 on v0

--- a/solution.py
+++ b/solution.py
@@ -24,8 +24,13 @@
     adapters = down_stack.shape[1] // RANK
     is_live, token_adapter = layout(lengths, adapter_ids, row_count)
     adapter_per_block = token_adapter.reshape(num_blocks, BLOCK)[:, 0]
-    w_piece = lax.all_gather(base_weight, "dp", axis=0, tiled=True)
-    a_piece = lax.all_gather(down_stack, "dp", axis=0, tiled=True)
+    w_piece, a_piece = jnp.split(
+        lax.all_gather(
+            jnp.concatenate([base_weight, down_stack], axis=1), "dp", axis=0, tiled=True
+        ),
+        [base_weight.shape[1]],
+        axis=1,
+    )
     width_dev = w_piece.shape[0]
     base_projection_share = jnp.dot(tokens, w_piece, preferred_element_type=jnp.float32)
     down_split = a_piece.reshape(width_dev, adapters, RANK)

time: 209 us -> 162 us (0.78)
  waiting for transfers between devices: 160 us -> 105 us
  local copies, waits for them, and re-layouts: 10.8 us -> 18.6 us
    all_gather x2 -> x1, waiting for transfers between devices: 160 us -> 105 us  [local(): lax.all_gather(jnp.concatenate([base_weight, down_stack], axis=1), 'dp',...]
    split x0 -> x1, local copies, waits for them, and re-layouts: none -> 7.64 us  [local(): jnp.split(lax.all_gather(jnp.concatenate([base_weight, down_stack], axis=...]
  transfers between devices with their start and end apart: 2 -> 1, of which waited for: 2 -> 1; matrix products, arithmetic and copies ran while one was open for 10% -> 4% of each run, Pallas kernels for 0% -> 0%
where the time goes in v1:
time: 162 us
  waiting for transfers between devices  105 us (65%)
  local copies, waits for them, and re-layouts  18.6 us (11%)
  matrix products  17.8 us (11%)
  between operations  13.6 us (8%)
  other arithmetic  6.42 us (4%)
    all_gather x1, waiting for transfers between devices, local(): lax.all_gather(jnp.concatenate([base_weight, down_stack], axis=1), 'dp',...  105 us
    dot_general x1, matrix products, local(): jnp.dot(tokens, w_piece, preferred_element_type=jnp.float32)  11.1 us
    split x1, local copies, waits for them, and re-layouts, local(): jnp.split(lax.all_gather(jnp.concatenate([base_weight, down_stack], axis=...  7.64 us
    dot_general x1, matrix products, local(): jnp.einsum('wmu,uwi->wmi', token_block_groups, selected_adapter, preferre...  6.06 us
    gather x1, local copies, waits for them, and re-layouts, local(): selected_adapter = jnp.take(down_split, adapter_per_block, axis=1)  5.88 us
  transfers between devices with their start and end apart: 1, of which 1 were waited for; matrix products, arithmetic and copies ran while one was open for 4% of the time, Pallas kernels for 0%

profile of v1, /device:TPU:0, one launch (start us, length us, event | category | flops | bytes accessed | tf_op | source)
XLA Modules:
  0.0 161.5 jit_solution(14305481152199127468)
XLA Ops:
  6.5 0.0 copy-start
  6.5 0.0 copy-start.2
  6.5 0.0 copy-start.1
  6.5 0.0 copy-start.3
  6.5 0.0 all-gather.2.cloned.1.call-start
  6.6 1.3 copy.11
  7.9 1.4 copy.10
  9.3 1.2 pad_maximum_fusion
  10.5 0.0 all-gather.2.cloned.1.call-update
  10.5 0.0 copy-done.2
  10.6 0.0 copy-done.1
  10.6 0.6 fusion.23
  11.2 1.3 fusion.21
  12.5 1.3 and_bitcast_fusion
  13.7 0.7 fusion.22
  14.4 1.3 select_compare_fusion
  15.7 1.3 fusion.19
  17.0 0.0 copy-done.3
  17.0 0.1 select_reduce_fusion
  17.1 105.1 %all-gather.2.cloned.1.call-done = bf16[8192,1280]{0,1:T(8,128)(2,1)} async-done(((bf16[512,1280]{0,1:T(8,128)(2,1)}), bf16[8192,1280]{0,1:T(8,128)(2,1)}) %all-gather.2.cloned.1.call-update) | async-done | bytes 20971536 | tf_op jit(solution)/shard_map/all_gather | solution.py:28
  122.2 7.6 %split.9 = bf16[8192,512]{0,1:T(8,128)(2,1)} slice(bf16[8192,1280]{0,1:T(8,128)(2,1)} %all-gather.2.cloned.1.call-done), slice={[0:8192], [768:1280]} | slice | bytes 16777216 | tf_op jit(solution)/shard_map/split | solution.py:27
  129.8 5.9 %gather_fusion = bf16[3,8192,64]{1,2,0:T(8,128)(2,1)} fusion(bf16[8192,8,64]{0,2,1:T(8,128)(2,1)} %bitcast.32, s32[1024]{0:T(1024)S(1)} %pad_clamp_fusion), kind=kCustom, calls=%fused_computation | custom fusion | bytes 6291468 | tf_op jit(solution)/shard_map/jit(_take)/gather | solution.py:37
  135.7 6.1 %fusion.16 = bf16[3,8,8,128]{3,2,1,0:T(8,128)(2,1)S(1)} fusion(bf16[3,128,8192]{2,1,0:T(8,128)(2,1)} %bitcast.35, bf16[3,8192,64]{1,2,0:T(8,128)(2,1)} %gather_fusion, pred[3]{0:T(512)(128)(4,1)S(1)} %and_bitcast_fusion), kind=kOutput, calls=%fused_computation.15 | convolution fusion | flops 404250624 | bytes 9486339 | tf_op jit(solution)/shard_map/wmu,uwi->wmi/dot_general | solution.py:39
  141.8 0.1 broadcast_select_fusion
  141.8 11.1 %fusion.7 = f32[384,768]{0,1:T(8,128)S(1)} fusion(bf16[384,8192]{1,0:T(8,128)(2,1)} %param.7, bf16[8192,1280]{0,1:T(8,128)(2,1)} %all-gather.2.cloned.1.call-done), kind=kOutput, calls=%fused_computation.8 | convolution fusion | flops 4831838208 | bytes 20054016 | tf_op jit(solution)/shard_map/dot_general | solution.py:35
  153.0 0.0 copy-done
  153.0 0.6 fusion.12
  153.6 1.1 copy.14
  (4 shorter events, 0.0 us)
Async XLA Ops:
  6.5 146.4 %copy-start = (bf16[512,768]{1,0:T(8,128)(2,1)S(1)}, bf16[512,768]{1,0:T(8,128)(2,1)}, u32[]{:S(2)}) copy-start(bf16[512,768]{1,0:T(8,128)(2,1)} %param.10) | copy-start | bytes 2359300
  6.5 4.0 %copy-start.2 = (s32[2]{0:T(128)S(1)}, s32[2]{0:T(128)}, u32[]{:S(2)}) copy-start(s32[2]{0:T(128)} %param.12) | copy-start | bytes 28
  6.5 4.0 %copy-start.1 = (s32[2]{0:T(128)S(1)}, s32[2]{0:T(128)}, u32[]{:S(2)}) copy-start(s32[2]{0:T(128)} %param.13) | copy-start | bytes 28
  6.5 10.4 %copy-start.3 = (f32[8]{0:T(128)S(1)}, f32[8]{0:T(128)}, u32[]{:S(2)}) copy-start(f32[8]{0:T(128)} %param.11) | copy-start | bytes 100
  6.5 115.6 %all-gather.2.cloned.1.call-start = ((), (), s32[]{:S(2)}) async-start(), calls=%async_computation | async-start | bytes 22282240 | tf_op jit(solution)/shard_map/all_gather | solution.py:28
Sparse Core Ops, SparseCore 0:
  10.6 111.4 all-gather.1
